TPU v7x, 32 devices: a whole 2x2x4 slice. The times are simulated.
32 devices in a mesh: lon: 8 (over z, x), lat: 4 (over y, core).
Axes of the slice: x: 2, y: 2, z: 4, core: 2. Of those that a mesh axis runs over, the one named last changes fastest.
Arguments:
- grid_field: float32 [4, 64, 16, 2048], P(None, 'lat', None, 'lon'), may hold values from -6 to 6
- lat_weight: float32 [64], replicated, may hold values from 0.3 to 3
Outputs:
- spec_real: float32 [4, 64, 16, 1024], P(None, None, 'lat', 'lon')
- spec_imag: float32 [4, 64, 16, 1024], P(None, None, 'lat', 'lon')
All inputs are finite; a program needn't handle non-finite values.
Results may differ from a plain program's by a relative error of at most 0.000071.
Values sent between devices are 32-bit elements; how exact they have to be, the bound alone decides.
A program may use at most 64 MiB of HBM per device.

v0:
```python
import math
import jax
import jax.numpy as jnp
from jax import lax
from jax.sharding import PartitionSpec as P

MODES = 1024
two_pi = 2.0 * math.pi


def mode_table(lon_ids, mode_ids, length):
    phases = lon_ids[:, None] * mode_ids[None, :] % length
    angles = phases.astype(jnp.float32) * (two_pi / length)
    normalizer = 1.0 / math.sqrt(length)
    return (jnp.cos(angles) * normalizer, -jnp.sin(angles) * normalizer)


def per_device(grid_field, lat_weight):
    fields, lat_dev, radius_count, lon_dev = grid_field.shape
    cycle_size = lax.axis_size("lon")
    length = cycle_size * lon_dev
    mode_dev = MODES // cycle_size
    my_index = lax.axis_index("lon")
    row_count = fields * lat_dev * radius_count
    flat_grid = grid_field.reshape(row_count, lon_dev)
    mode_ids = my_index * mode_dev + jnp.arange(mode_dev, dtype=jnp.int32)
    lon_block = lax.all_gather(flat_grid, "lon", axis=1, tiled=True)
    lon_ids = jnp.arange(lon_block.shape[1], dtype=jnp.int32)
    cosine, sine_part = mode_table(lon_ids, mode_ids, length)
    dft_table = jnp.concatenate([cosine, sine_part], axis=1)
    summed = jnp.dot(
        lon_block, dft_table, precision=lax.Precision.HIGHEST, preferred_element_type=jnp.float32
    )
    spectra = summed.reshape(fields, lat_dev, radius_count, 2, mode_dev)
    gathered = lax.all_to_all(spectra, "lat", split_axis=2, concat_axis=1, tiled=True)
    weights_row = lat_weight[None, :, None, None]
    return (gathered[:, :, :, 0, :] * weights_row, gathered[:, :, :, 1, :] * weights_row)


def solution(mesh):
    in_specs = (P(None, "lat", None, "lon"), P())
    out_specs = (P(None, None, "lat", "lon"), P(None, None, "lat", "lon"))
    return jax.shard_map(
        per_device, mesh=mesh, in_specs=in_specs, out_specs=out_specs, check_vma=False
    )
```

profile of v0, /device:TPU:0, one launch (start us, length us, event | category | flops | bytes accessed | tf_op | source)
XLA Modules:
  0.0 181.7 jit_solution(17533059803057809148)
XLA Ops:
  7.2 0.0 all-gather.2.cloned.1.call-start
  7.2 0.7 all-gather.2.cloned.1.call-update
  7.9 4.2 %cosine_multiply_fusion = (f32[2048,128]{1,0:T(8,128)S(1)}, f32[2048,128]{1,0:T(8,128)S(1)}) fusion(s32[128]{0:T(128)S(1)} %iota_add_fusion), kind=kLoop, calls=%fused_computation.12 | loop fusion | flops 4456448 | bytes 2097664 | tf_op jit(solution)/shard_map/mul | solution.py:15
  12.1 125.6 %all-gather.2.cloned.1.call-done = f32[1024,2048]{1,0:T(8,128)} async-done(((f32[1024,256]{1,0:T(8,128)}), f32[1024,2048]{1,0:T(8,128)}) %all-gather.2.cloned.1.call-update) | async-done | bytes 8388624 | tf_op jit(solution)/shard_map/all_gather | solution.py:27
  137.7 15.9 %fusion.4 = f32[1024,256]{0,1:T(8,128)S(1)} fusion(f32[1024,2048]{1,0:T(8,128)} %all-gather.2.cloned.1.call-done, f32[2048,128]{1,0:T(8,128)S(1)} %get-tuple-element.9, f32[2048,128]{1,0:T(8,128)S(1)} %get-tuple-element.8), kind=kOutput, calls=%fused_computation.7 | convolution fusion | flops 6442975232 | bytes 11534336 | tf_op jit(solution)/shard_map/dot_general | solution.py:31
  153.6 0.0 copy-start
  153.6 0.3 copy.13
  154.0 0.5 reshape.16
  154.5 0.6 copy.14
  155.1 17.0 %all_to_all.18 = f32[4,16,16,2,128]{4,3,1,0,2:T(2,128)S(1)} all-to-all(f32[4,16,16,2,128]{4,3,1,0,2:T(2,128)S(1)} %copy.14), channel_id=1, replica_groups=mesh['lon'=8,'lat'=4] {'lat'}, dimensions={2} | all-to-all | bytes 2097152 | tf_op jit(solution)/shard_map/all_to_all | solution.py:35
  172.1 0.1 copy.15
  172.2 0.1 copy.16
  172.4 0.0 copy-done
  172.4 0.2 fusion.13
  172.6 1.1 copy.19
  173.7 1.1 copy.18
  (1 shorter events, 0.0 us)
Async XLA Ops:
  7.2 130.5 %all-gather.2.cloned.1.call-start = ((), (), s32[]{:S(2)}) async-start(), calls=%async_computation.1 | async-start | bytes 9437184 | tf_op jit(solution)/shard_map/all_gather | solution.py:27
  153.6 18.8 %copy-start = (f32[64]{0:T(128)S(1)}, f32[64]{0:T(128)}, u32[]{:S(2)}) copy-start(f32[64]{0:T(128)} %param.3) | copy-start | bytes 772
Sparse Core Ops, SparseCore 0:
  10.0 127.6 all-gather.1
where the time goes:
time: 182 us
  waiting for transfers between devices  126 us (69%)
  blocking collectives  17 us (9%)
  matrix products  15.9 us (9%)
  between operations  14.1 us (8%)
  other arithmetic  4.36 us (2%)
  local copies, waits for them, and re-layouts  3.95 us (2%)
    all_gather x1, waiting for transfers between devices, per_device(): lon_block = lax.all_gather(flat_grid, 'lon', axis=1, tiled=True)  126 us
    all_to_all x1, blocking collectives, per_device(): lax.all_to_all(spectra, 'lat', split_axis=2, concat_axis=1, tiled=True)  17 us
    dot_general x1, matrix products, per_device(): jnp.dot(lon_block, dft_table, precision=lax.Precision.HIGHEST, preferred_...  15.9 us
    mul x1, other arithmetic, mode_table(): return (jnp.cos(angles) * normalizer, -jnp.sin(angles) * normalizer)  4.17 us
  transfers between devices with their start and end apart: 1, of which 1 were waited for; matrix products, arithmetic and copies ran while one was open for 2% of the time, Pallas kernels for 0%

commit v1 on v0

--- a/solution.py
+++ b/solution.py
@@ -24,7 +24,9 @@
     row_count = fields * lat_dev * radius_count
     flat_grid = grid_field.reshape(row_count, lon_dev)
     mode_ids = my_index * mode_dev + jnp.arange(mode_dev, dtype=jnp.int32)
-    lon_block = lax.all_gather(flat_grid, "lon", axis=1, tiled=True)
+    lon_block = jnp.concatenate(
+        lax.all_to_all(jnp.stack([flat_grid] * lax.axis_size("lon")), "lon", 0, 0), axis=1
+    )
     lon_ids = jnp.arange(lon_block.shape[1], dtype=jnp.int32)
     cosine, sine_part = mode_table(lon_ids, mode_ids, length)
     dft_table = jnp.concatenate([cosine, sine_part], axis=1)

time: 182 us -> 228 us (1.25)
  waiting for transfers between devices: 126 us -> 179 us
  between operations: 14.1 us -> 0.72 us
  starting transfers between devices: 0.04 us -> 7.28 us
  matrix products: 15.9 us -> 9.61 us
  local copies, waits for them, and re-layouts: 3.95 us -> 9.78 us
    all_to_all x0 -> x1, waiting for transfers between devices: none -> 179 us  [per_device(): lax.all_to_all(jnp.stack([flat_grid] * lax.axis_size('lon')), 'lon', 0, 0)]
    all_gather x1 -> x0, waiting for transfers between devices: 126 us -> none  [per_device(): lon_block = lax.all_gather(flat_grid, 'lon', axis=1, tiled=True)]
    all_to_all x0 -> x1, starting transfers between devices: none -> 7.28 us  [per_device(): lax.all_to_all(jnp.stack([flat_grid] * lax.axis_size('lon')), 'lon', 0, 0)]
    dot_general x1, matrix products: 15.9 us -> 9.61 us  [per_device(): jnp.dot(lon_block, dft_table, precision=lax.Precision.HIGHEST, preferred_...]
    another operation x0 -> x2, local copies, waits for them, and re-layouts: none -> 5.84 us  [per_device(): jnp.stack([flat_grid] * lax.axis_size('lon'))]
where the time goes in v1:
time: 228 us
  waiting for transfers between devices  179 us (79%)
  blocking collectives  17 us (7%)
  local copies, waits for them, and re-layouts  9.78 us (4%)
  matrix products  9.61 us (4%)
  starting transfers between devices  7.28 us (3%)
  other arithmetic  4.36 us (2%)
    all_to_all x1, waiting for transfers between devices, per_device(): lax.all_to_all(jnp.stack([flat_grid] * lax.axis_size('lon')), 'lon', 0, 0)  179 us
    all_to_all x1, blocking collectives, per_device(): lax.all_to_all(spectra, 'lat', split_axis=2, concat_axis=1, tiled=True)  17 us
    dot_general x1, matrix products, per_device(): jnp.dot(lon_block, dft_table, precision=lax.Precision.HIGHEST, preferred_...  9.61 us
    all_to_all x1, starting transfers between devices, per_device(): lax.all_to_all(jnp.stack([flat_grid] * lax.axis_size('lon')), 'lon', 0, 0)  7.28 us
    another operation x2, local copies, waits for them, and re-layouts, per_device(): jnp.stack([flat_grid] * lax.axis_size('lon'))  5.84 us
  transfers between devices with their start and end apart: 1, of which 1 were waited for; matrix products, arithmetic and copies ran while one was open for 2% of the time, Pallas kernels for 0%

profile of v1, /device:TPU:0, one launch (start us, length us, event | category | flops | bytes accessed | tf_op | source)
XLA Modules:
  0.0 227.8 jit_solution(13551627884268721358)
XLA Ops:
  0.6 1.6 copy.15
  2.2 4.3 %stack.3 = f32[8,1024,256]{1,2,0:T(8,128)} broadcast(f32[1024,256]{0,1:T(8,128)S(1)} %copy.15), dimensions={1,2} | broadcast | bytes 9437184 | tf_op jit(solution)/shard_map/stack | solution.py:28
  6.5 7.3 %all-to-all-start = ((f32[8,1024,256]{1,2,0:T(8,128)}), f32[8,1024,256]{1,2,0:T(8,128)}, u32[]{:S(2)}, u32[]{:S(2)}) async-start(f32[8,1024,256]{1,2,0:T(8,128)} %stack.3), calls=%async_computation | async-start | bytes 16777216 | tf_op jit(solution)/shard_map/all_to_all | solution.py:28
  13.8 4.2 %cosine_multiply_fusion = (f32[2048,128]{1,0:T(8,128)S(1)}, f32[2048,128]{1,0:T(8,128)S(1)}) fusion(s32[128]{0:T(128)S(1)} %iota_add_fusion), kind=kLoop, calls=%fused_computation.12 | loop fusion | flops 4456448 | bytes 2097664 | tf_op jit(solution)/shard_map/mul | solution.py:15
  17.9 179.0 %all-to-all-done = f32[8,1024,256]{1,2,0:T(8,128)} async-done(((f32[8,1024,256]{1,2,0:T(8,128)}), f32[8,1024,256]{1,2,0:T(8,128)}, u32[]{:S(2)}, u32[]{:S(2)}) %all-to-all-start) | async-done | bytes 8388640 | tf_op jit(solution)/shard_map/all_to_all | solution.py:28
  196.9 9.6 %fusion.4 = f32[1024,256]{0,1:T(8,128)S(1)} fusion(f32[1024,2048]{0,1:T(8,128)} %bitcast.2, f32[2048,128]{1,0:T(8,128)S(1)} %get-tuple-element.9, f32[2048,128]{1,0:T(8,128)S(1)} %get-tuple-element.8), kind=kOutput, calls=%fused_computation.7 | convolution fusion | flops 6442975232 | bytes 11534336 | tf_op jit(solution)/shard_map/dot_general | solution.py:33
  206.5 0.0 copy-start
  206.6 0.3 copy.16
  206.9 0.5 reshape.22
  207.4 0.6 copy.17
  208.0 17.0 %all_to_all.23 = f32[4,16,16,2,128]{4,3,1,0,2:T(2,128)S(1)} all-to-all(f32[4,16,16,2,128]{4,3,1,0,2:T(2,128)S(1)} %copy.17), channel_id=1, replica_groups=mesh['lon'=8,'lat'=4] {'lat'}, dimensions={2} | all-to-all | bytes 2097152 | tf_op jit(solution)/shard_map/all_to_all | solution.py:37
  225.1 0.1 copy.18
  225.1 0.1 copy.19
  225.3 0.0 copy-done
  225.3 0.2 fusion.13
  225.5 1.1 copy.21
  226.6 1.1 copy.22
  (1 shorter events, 0.0 us)
Async XLA Ops:
  6.5 190.4 %all-to-all-start = ((f32[8,1024,256]{1,2,0:T(8,128)}), f32[8,1024,256]{1,2,0:T(8,128)}, u32[]{:S(2)}, u32[]{:S(2)}) async-start(f32[8,1024,256]{1,2,0:T(8,128)} %stack.3), calls=%async_computation | async-start | bytes 16777216 | tf_op jit(solution)/shard_map/all_to_all | solution.py:28
  206.5 18.7 %copy-start = (f32[64]{0:T(128)S(1)}, f32[64]{0:T(128)}, u32[]{:S(2)}) copy-start(f32[64]{0:T(128)} %param.3) | copy-start | bytes 772
